TPU v7x, 32 devices: a whole 2x2x4 slice. The times are simulated.
32 devices in a mesh: seq: 4 (over z), head: 8 (over y, x, core).
Axes of the slice: x: 2, y: 2, z: 4, core: 2. Of those that a mesh axis runs over, the one named last changes fastest.
Arguments:
- query: float32 [3072, 1024], P('seq', 'head'), may hold values from -6 to 6
- key_in: float32 [3072, 1024], P('seq', 'head'), may hold values from -6 to 6
- value: float32 [3072, 1024], P('seq', 'head'), may hold values from -6 to 6
- out_grad: float32 [3072, 1024], P('seq', 'head'), may hold values from -6 to 6
- head_scale: float32 [8], P('head'), may hold values from 0.5 to 2
- norm_gain: float32 [1024], P('head'), may hold values from 0.5 to 1.5
- group_counts: int32 [4], replicated, may hold values from 1 to 6, 12 in all
Outputs:
- normed: float32 [3072, 1024], P('seq', 'head')
- grad_query: float32 [3072, 1024], P('seq', 'head')
- grad_key: float32 [3072, 1024], P('seq', 'head')
- grad_value: float32 [3072, 1024], P('seq', 'head')
Inputs may be any that keep to these rules, and one draw needn't show every extreme that they name: The live rows of shard i are its first 128 * group_counts[i] rows; the counts sum to 3 * 4 and the largest is exactly 6.
All inputs are finite; a program needn't handle non-finite values.
Results may differ from a plain program's by a relative error of at most 0.0001.
Values sent between devices are 32-bit elements; how exact they have to be, the bound alone decides.
A program may use at most 64 MiB of HBM per device.

v0:
```python
import functools

import jax
import jax.numpy as jnp
from jax import lax
from jax.experimental import pallas as pl
from jax.experimental.pallas import tpu as pltpu
from jax.sharding import PartitionSpec as P

GROUP = 128
CHUNKS = 4
EPS = 1e-05
F32 = jnp.float32
BF16 = jnp.bfloat16
NN = (((1,), (0,)), ((), ()))
NT = (((1,), (1,)), ((), ()))
TN = (((0,), (0,)), ((), ()))


def dot(left, right, dims):
    return lax.dot_general(left, right, dims, preferred_element_type=F32)


def split(x):
    high = x.astype(BF16)
    low = (x - high.astype(F32)).astype(BF16)
    return high, low


def rows_by_rows(a, b):
    left = jnp.concatenate([a[0], a[1], a[0]], axis=1)
    right = jnp.concatenate([b[0], b[0], b[1]], axis=1)
    return dot(left, right, NT)


def times(a, b):
    d = b[0].shape[1]
    both = dot(a[0], jnp.concatenate([b[0], b[1]], axis=1), NN)
    return both[:, :d] + both[:, d:] + dot(a[1], b[0], NN)


def times_state(a, s):
    d = s[0].shape[1]
    left = jnp.concatenate([a[0], a[1]], axis=1)
    top = jnp.concatenate([s[0], s[1]], axis=1)
    bottom = jnp.concatenate([s[0], jnp.zeros_like(s[0])], axis=1)
    both = dot(left, jnp.concatenate([top, bottom], axis=0), NN)
    return both[:, :d] + both[:, d:]


def times_state_t(a, s):
    d = s[0].shape[0]
    left = jnp.concatenate([a[0], a[1]], axis=1)
    top = jnp.concatenate([s[0], s[0]], axis=1)
    bottom = jnp.concatenate([s[1], jnp.zeros_like(s[1])], axis=1)
    both = dot(left, jnp.concatenate([top, bottom], axis=0), NT)
    return both[:, :d] + both[:, d:]


def outer(a, b):
    d = a[0].shape[1]
    full = dot(jnp.concatenate(a, axis=1), jnp.concatenate(b, axis=1), TN)
    return full[:d, :d] + full[:d, d:] + full[d:, :d] + full[d:, d:]


def row_sums(x):
    high, low = split(x)
    low2 = (x - high.astype(F32) - low.astype(F32)).astype(BF16)
    parts = jnp.concatenate([high, low, low2], axis=1)
    return dot(jnp.ones((8, parts.shape[1]), BF16), parts, NT)[0:1]


def kernel(
    n_seq, n_head, block, head_scale, counts_hbm,
    q_hbm, k_hbm, v_hbm, g_hbm, gain_hbm,
    normed, gq, gk, gv, k_h, k_l, v_h, v_l, t_out,
    counts, q_in, k_in, v_in, g_in, gain,
    q_h, q_l, o_h, o_l, p_h, p_l,
    scaled, send_s, recv_s, send_t, recv_t, end_s, end_t, sums, sums_in,
    in_sem, s_send, s_recv, t_send, t_recv, h_send, h_recv, e_send, e_recv,
):
    cap, d = q_in.shape
    blocks = cap // block
    per = block // GROUP
    pos = lax.axis_index("seq")
    head = lax.axis_index("head")
    half = sums.shape[0] // 2

    loads = [
        pltpu.make_async_copy(src, dst, in_sem.at[i])
        for i, (src, dst) in enumerate(
            (
                (counts_hbm, counts), (k_hbm, k_in), (v_hbm, v_in), (q_hbm, q_in),
                (g_hbm, g_in), (gain_hbm, gain),
            )
        )
    ]
    for load in loads:
        load.start()

    first, last = pos == 0, pos == n_seq - 1
    barrier = pltpu.get_barrier_semaphore()

    direct = n_seq == 4

    def greet(other):
        pl.semaphore_signal(barrier, inc=1, device_id={"seq": other}, device_id_type=pl.DeviceIdType.MESH)

    seq_peers = 0
    for delta in (-2, -1, 1, 2):
        there = jnp.logical_and(pos + delta >= 0, pos + delta < n_seq)

        @pl.when(there)
        def _():
            greet(pos + delta)

        seq_peers = seq_peers + jnp.where(there, 1, 0)

    for step in range(1, n_head):
        pl.semaphore_signal(
            barrier, inc=1, device_id={"head": lax.rem(head + step, n_head)},
            device_id_type=pl.DeviceIdType.MESH,
        )

    loads[0].wait()
    live = counts[pos] * GROUP
    row = lax.broadcasted_iota(jnp.int32, (block, d), 0)
    t_row = lax.broadcasted_iota(jnp.int32, (block, block), 0)
    t_col = lax.broadcasted_iota(jnp.int32, (block, block), 1)

    def take(b):
        return pl.ds(b * block, block)

    def pair(high, low, b):
        return high[take(b), :], low[take(b), :]

    def keep(source, high, low, b):
        x = jnp.where(row + b * block < live, source[take(b), :], 0.0)
        high[take(b), :], low[take(b), :] = split(x)

    sums[...] = jnp.zeros_like(sums)
    loads[1].wait()
    loads[2].wait()
    states = []
    for b in range(blocks):
        keep(k_in, k_h, k_l, b)
        keep(v_in, v_h, v_l, b)
        states.append(outer(pair(k_h, k_l, b), pair(v_h, v_l, b)))
    before = [jnp.zeros((d, d), F32)]
    for b in range(blocks):
        before.append(before[-1] + states[b])

    def piece(c):
        return pl.ds(c * (d // CHUNKS), d // CHUNKS)

    def hop(src, dst, s_sem, r_sem, c, target):
        return pltpu.make_async_remote_copy(
            src_ref=src.at[piece(c), :], dst_ref=dst.at[piece(c), :],
            send_sem=s_sem.at[c], recv_sem=r_sem.at[c],
            device_id={"seq": target}, device_id_type=pl.DeviceIdType.MESH,
        )

    def far(src, dst, s_sem, r_sem, target):
        return pltpu.make_async_remote_copy(
            src_ref=src, dst_ref=dst, send_sem=s_sem, recv_sem=r_sem,
            device_id={"seq": target}, device_id_type=pl.DeviceIdType.MESH,
        )

    def part(ref, c):
        return ref.at[piece(c), :]

    def exchange(way, src, dst, end, s_sem, r_sem):
        delta = 1 if way == 0 else -1
        order = pos if way == 0 else n_seq - 1 - pos
        first, last = order == 0, order == n_seq - 1

        def neighbour(c):
            return hop(src, dst, s_sem, r_sem, c, pos + delta)

        def skip(c):
            return far(part(src, c), part(dst, c), e_send.at[way, c], r_sem.at[c], pos + 2 * delta)

        def own():
            return far(src, end, e_send.at[way, CHUNKS], e_recv.at[way, CHUNKS], pos + delta)

        def begin():
            @pl.when(first)
            def _():
                for c in range(CHUNKS):
                    neighbour(c).start()
                dst[...] = jnp.zeros_like(dst)

            if direct:

                @pl.when(order == 2)
                def _():
                    own().start()

        def relay():
            @pl.when(jnp.logical_not(first))
            def _():
                for c in range(CHUNKS):
                    neighbour(c).wait_recv()

                    @pl.when(order == 1 if direct else jnp.logical_not(last))
                    def _():
                        src[piece(c), :] += dst[piece(c), :]
                        if direct:
                            skip(c).start()
                        else:
                            neighbour(c).start()

                if direct:

                    @pl.when(order == 1)
                    def _():
                        for c in range(CHUNKS):
                            neighbour(c).start()

            if direct:

                @pl.when(last)
                def _():
                    own().wait_recv()
                    dst[...] += end[...]

        def close():
            @pl.when(order <= 1 if direct else jnp.logical_not(last))
            def _():
                for c in range(CHUNKS):
                    neighbour(c).wait_send()

            if direct:

                @pl.when(order == 1)
                def _():
                    for c in range(CHUNKS):
                        skip(c).wait_send()

                @pl.when(order == 2)
                def _():
                    own().wait_send()

        return begin, relay, close

    s_begin, s_relay, s_close = exchange(0, send_s, recv_s, end_s, s_send, s_recv)
    t_begin, t_relay, t_close = exchange(1, send_t, recv_t, end_t, t_send, t_recv)

    send_s[...] = before[-1]
    pl.semaphore_wait(barrier, n_head - 1 + seq_peers)

    s_begin()

    loads[3].wait()
    for b in range(blocks):
        keep(q_in, q_h, q_l, b)
        q_b, k_b = pair(q_h, q_l, b), pair(k_h, k_l, b)
        scores = jnp.where(t_row >= t_col, rows_by_rows(q_b, k_b), 0.0)
        scaled[take(b), :] = times(split(scores), pair(v_h, v_l, b))

    s_relay()

    loads[4].wait()
    loads[5].wait()
    scale = head_scale[0]
    gains = gain[...].reshape(1, d)
    for b in range(blocks):
        state = recv_s[...] + before[b]
        mine = (scaled[take(b), :] + times_state(pair(q_h, q_l, b), split(state))) * scale
        scaled[take(b), :] = mine
        square = row_sums(mine * mine)
        cross = row_sums(gains * g_in[take(b), :] * mine)
        for j in range(per):
            sums[b * per + j : b * per + j + 1, :] = square[:, j * GROUP : (j + 1) * GROUP]
            sums[half + b * per + j : half + b * per + j + 1, :] = cross[:, j * GROUP : (j + 1) * GROUP]

    shares = [
        pltpu.make_async_remote_copy(
            src_ref=sums, dst_ref=sums_in.at[step - 1],
            send_sem=h_send.at[step - 1], recv_sem=h_recv.at[step - 1],
            device_id={"head": lax.rem(head + step, n_head)},
            device_id_type=pl.DeviceIdType.MESH,
        )
        for step in range(1, n_head)
    ]
    for share in shares:
        share.start()

    for b in range(blocks):
        q_b, k_b = pair(q_h, q_l, b), pair(k_h, k_l, b)
        scores_t = jnp.where(t_row <= t_col, rows_by_rows(k_b, q_b), 0.0)
        p_h[take(b), :], p_l[take(b), :] = split(scores_t)

    total = sums[...]
    for step in range(1, n_head):
        shares[step - 1].wait_recv()
        total = total + sums_in[step - 1]
    features = d * n_head
    inverse = lax.rsqrt(total[:half] / features + EPS)
    factor = inverse * inverse * inverse * total[half:] / features
    columns = jnp.transpose(jnp.concatenate([inverse, factor], axis=0))

    t_states = []
    for b in range(blocks):
        inv = jnp.concatenate(
            [jnp.broadcast_to(columns[:, b * per + j : b * per + j + 1], (GROUP, d)) for j in range(per)], axis=0
        )
        fac = jnp.concatenate(
            [jnp.broadcast_to(columns[:, half + b * per + j : half + b * per + j + 1], (GROUP, d)) for j in range(per)],
            axis=0,
        )
        mine = scaled[take(b), :]
        weight = inv * gains
        normed[take(b), :] = mine * weight
        grad = (weight * g_in[take(b), :] - mine * fac) * scale
        grad = jnp.where(row + b * block < live, grad, 0.0)
        o_h[take(b), :], o_l[take(b), :] = split(grad)
        t_states.append(outer(pair(q_h, q_l, b), pair(o_h, o_l, b)))
    after = [jnp.zeros((d, d), F32)]
    for b in range(blocks - 1, -1, -1):
        after.append(after[-1] + t_states[b])
    after = after[::-1]

    send_t[...] = after[0]

    t_begin()
    for b in range(blocks):
        o_b, v_b = pair(o_h, o_l, b), pair(v_h, v_l, b)
        pulled = jnp.where(t_row >= t_col, rows_by_rows(o_b, v_b), 0.0)
        pulled_t = jnp.where(t_row <= t_col, rows_by_rows(v_b, o_b), 0.0)
        state = recv_s[...] + before[b]
        gq[take(b), :] = times_state_t(o_b, split(state)) + times(split(pulled), pair(k_h, k_l, b))
        gk[take(b), :] = times(split(pulled_t), pair(q_h, q_l, b))
        gv[take(b), :] = times(pair(p_h, p_l, b), o_b)

    t_relay()
    for b in range(blocks):
        t_out[b] = recv_t[...] + after[b + 1]

    for share in shares:
        share.wait_send()

    s_close()
    t_close()


def finish(
    block, normed, gq, gk, gv, k_h, k_l, v_h, v_l, t_in,
    normed_hbm, gq_hbm, gk_hbm, gv_hbm, gk_all, gv_all, sem,
):
    blocks = t_in.shape[0]
    stores = [
        pltpu.make_async_copy(normed, normed_hbm, sem.at[2 * blocks]),
        pltpu.make_async_copy(gq, gq_hbm, sem.at[2 * blocks + 1]),
    ]
    for store in stores:
        store.start()
    for b in range(blocks):
        rows = pl.ds(b * block, block)
        state = split(t_in[b])
        gk_all[rows, :] = gk[rows, :] + times_state_t((v_h[rows, :], v_l[rows, :]), state)
        gv_all[rows, :] = gv[rows, :] + times_state((k_h[rows, :], k_l[rows, :]), state)
        for i, (src, dst) in enumerate(((gk_all, gk_hbm), (gv_all, gv_hbm))):
            store = pltpu.make_async_copy(src.at[rows, :], dst.at[rows, :], sem.at[2 * b + i])
            store.start()
            stores.append(store)
    for store in stores:
        store.wait()


def on_device(n_seq, n_head, query, key_in, value, out_grad, head_scale, norm_gain, group_counts):
    cap, d = query.shape
    block = 2 * GROUP if cap % (2 * GROUP) == 0 else GROUP
    half = -(-(cap // GROUP) // 8) * 8
    blocks = cap // block
    hbm = pl.BlockSpec(memory_space=pltpu.HBM)
    vmem = pl.BlockSpec(memory_space=pltpu.VMEM)
    wide = pltpu.VMEM((cap, d), F32)
    narrow = pltpu.VMEM((cap, d), BF16)
    state = pltpu.VMEM((d, d), F32)
    rows = jax.ShapeDtypeStruct((cap, d), F32)
    rows_low = jax.ShapeDtypeStruct((cap, d), BF16)
    held = pl.pallas_call(
        functools.partial(kernel, n_seq, n_head, block),
        out_shape=[rows] * 4 + [rows_low] * 4 + [jax.ShapeDtypeStruct((blocks, d, d), F32)],
        in_specs=[pl.BlockSpec(memory_space=pltpu.SMEM)] + [hbm] * 6,
        out_specs=[vmem] * 9,
        scratch_shapes=[pltpu.SMEM(group_counts.shape, jnp.int32)]
        + [wide] * 4 + [pltpu.VMEM((d,), F32)]
        + [narrow] * 4 + [pltpu.VMEM((cap, block), BF16)] * 2
        + [wide]
        + [state] * 6
        + [pltpu.VMEM((2 * half, GROUP), F32), pltpu.VMEM((n_head - 1, 2 * half, GROUP), F32)]
        + [pltpu.SemaphoreType.DMA((6,))]
        + [pltpu.SemaphoreType.DMA((CHUNKS,))] * 4
        + [pltpu.SemaphoreType.DMA((n_head - 1,))] * 2
        + [pltpu.SemaphoreType.DMA((2, CHUNKS + 1)), pltpu.SemaphoreType.DMA((2, CHUNKS + 1))],
        compiler_params=pltpu.CompilerParams(
            collective_id=0, has_side_effects=True, vmem_limit_bytes=32 * 1024 * 1024
        ),
    )(head_scale, *(
        pltpu.with_memory_space_constraint(x, pltpu.HBM)
        for x in (group_counts, query, key_in, value, out_grad, norm_gain)
    ))
    return pl.pallas_call(
        functools.partial(finish, block),
        out_shape=[rows] * 4,
        in_specs=[vmem] * 9,
        out_specs=[hbm] * 4,
        scratch_shapes=[wide] * 2 + [pltpu.SemaphoreType.DMA((2 * blocks + 2,))],
        compiler_params=pltpu.CompilerParams(vmem_limit_bytes=32 * 1024 * 1024),
    )(*held)


def solution(mesh):
    rows = P("seq", "head")
    return jax.shard_map(
        functools.partial(on_device, mesh.shape["seq"], mesh.shape["head"]),
        mesh=mesh,
        in_specs=(rows, rows, rows, rows, P("head"), P("head"), P()),
        out_specs=(rows, rows, rows, rows),
        check_vma=False,
    )
```

profile of v0, /device:TPU:0, one launch (start us, length us, event | category | flops | bytes accessed | tf_op | source)
XLA Modules:
  0.0 26.1 jit_solution(5863390534256920617)
XLA Ops:
  1.3 23.6 %shard_map.102 = (f32[768,128]{1,0:T(8,128)S(1)}, f32[768,128]{1,0:T(8,128)S(1)}, f32[768,128]{1,0:T(8,128)S(1)}, f32[768,128]{1,0:T(8,128)S(1)}, bf16[768,128]{...) custom-call(f32[1]{0:T(128)S(6)} %copy.11.head_scale, ...), custom_call_target="tpu_custom_call" | custom-call | tf_op jit(solution)/shard_map/pallas_call | solution.py:383
  24.9 1.2 %shard_map.103 = (f32[768,128]{1,0:T(8,128)}, f32[768,128]{1,0:T(8,128)}, f32[768,128]{1,0:T(8,128)}, f32[768,128]{1,0:T(8,128)}) custom-call(f32[768,128]{1,0:T(8,128)S(1)} %get-tuple-element.13.normed, f32[768,128]{1,0:T(8,128)S(1)} %get-tuple-element.14.gq, f32[768,128]{1,0:T(8,128)S(1)} %get-tuple-element.15.gk, f32[768,128]{1,0:T(8,128)S(1)} %get-tuple-element.16.gv, ...), custom_call_target="tpu_custom_call" | custom-call | tf_op jit(solution)/shard_map/pallas_call | solution.py:405
where the time goes:
time: 26.3 us; the launch traced here: 26.1 us
  Pallas kernels  24.8 us (94%)
  between operations  1.29 us (5%)
    pallas_call x1, Pallas kernels, on_device(): pl.pallas_call(functools.partial(kernel, n_seq, n_head, block), out_shape...  23.6 us
    pallas_call x1, Pallas kernels, on_device(): pl.pallas_call(functools.partial(finish, block), out_shape=[rows] * 4, in...  1.2 us

commit v1 on v0

v1 whole, which is shorter than its diff:
```python
import functools

import jax
import jax.numpy as jnp
from jax import lax
from jax.experimental import pallas as pl
from jax.experimental.pallas import tpu as pltpu
from jax.sharding import PartitionSpec as P

GROUP = 128
EPS = 1e-05
F32 = jnp.float32
BF16 = jnp.bfloat16
MESH = pl.DeviceIdType.MESH
NN = (((1,), (0,)), ((), ()))
NT = (((1,), (1,)), ((), ()))
TN = (((0,), (0,)), ((), ()))


def dot(left, right, dims):
    return lax.dot_general(left, right, dims, preferred_element_type=F32)


def split(x):
    high = x.astype(BF16)
    low = (x - high.astype(F32)).astype(BF16)
    return high, low


def beside(pair):
    return jnp.concatenate(pair, axis=1)


def add_rows(x):
    half = x.shape[0] // 2
    return x[:half] + x[half:]


def add_columns(x):
    half = x.shape[1] // 2
    return x[:, :half] + x[:, half:]


def stacked(s):
    top = jnp.concatenate([s[0], s[0]], axis=1)
    bottom = jnp.concatenate([s[1], jnp.zeros_like(s[1])], axis=1)
    return jnp.concatenate([top, bottom], axis=0)


def rows_by_rows(a, b):
    left = jnp.concatenate([a[0], a[1], a[0]], axis=1)
    right = jnp.concatenate([b[0], b[0], b[1]], axis=1)
    return dot(left, right, NT)


def rows_by_columns(a, b):
    left = jnp.concatenate([a[0], a[1], a[0]], axis=1)
    right = jnp.concatenate([b[0], b[0], b[1]], axis=0)
    return dot(left, right, NN)


def times(a, b):
    return add_columns(dot(a[0], beside(b), NN)) + dot(a[1], b[0], NN)


def columns_times(a, b):
    return add_columns(dot(a[0], beside(b), TN)) + dot(a[1], b[0], TN)


def times_state(a, s):
    top = jnp.concatenate([s[0], s[1]], axis=1)
    bottom = jnp.concatenate([s[0], jnp.zeros_like(s[0])], axis=1)
    return add_columns(dot(beside(a), jnp.concatenate([top, bottom], axis=0), NN))


def times_state_t(a, s):
    return add_columns(dot(beside(a), stacked(s), NT))


def state_by_rows(s, a):
    return add_rows(dot(s, beside(a), NT))


def outer(a, b):
    return add_rows(add_columns(dot(beside(a), beside(b), TN)))


def kernel(
    n_seq, n_head, block, head_scale, counts_hbm,
    q_hbm, k_hbm, v_hbm, g_hbm, gain_hbm,
    normed, gq, gk, gv, k_h, k_l, v_h, v_l, t_out,
    counts, q_in, k_in, v_in, g_in, gain,
    q_h, q_l, p_h, p_l, mine_t, gg_t, o_h, o_l,
    send_s, recv_s, send_t, recv_t, sums, sums_in,
    in_sem, s_send, s_recv, t_send, t_recv, h_send, h_recv,
):
    cap, d = q_in.shape
    blocks = cap // block
    per = block // GROUP
    pos = lax.axis_index("seq")
    head = lax.axis_index("head")
    half = sums.shape[0] // 2

    barrier = pltpu.get_barrier_semaphore()
    for step in range(1, n_seq):
        pl.semaphore_signal(barrier, inc=1, device_id={"seq": lax.rem(pos + step, n_seq)}, device_id_type=MESH)
    loads = [
        pltpu.make_async_copy(src, dst, in_sem.at[i])
        for i, (src, dst) in enumerate(
            (
                (counts_hbm, counts), (k_hbm, k_in), (v_hbm, v_in), (q_hbm, q_in),
                (g_hbm, g_in), (gain_hbm, gain),
            )
        )
    ]
    for load in loads:
        load.start()
    for step in range(1, n_head):
        pl.semaphore_signal(barrier, inc=1, device_id={"head": lax.rem(head + step, n_head)}, device_id_type=MESH)

    def exchange(way, src, dst, s_sem, r_sem):
        order = pos if way == 1 else n_seq - 1 - pos
        to_last = n_seq - 1 - order

        def message(reach):
            return pltpu.make_async_remote_copy(
                src_ref=src, dst_ref=dst.at[reach - 1],
                send_sem=s_sem.at[reach - 1], recv_sem=r_sem.at[reach - 1],
                device_id={"seq": pos + way * reach}, device_id_type=MESH,
            )

        def clear():
            for reach in range(1, n_seq):

                @pl.when(order < reach)
                def _():
                    dst[reach - 1] = jnp.zeros(dst.shape[1:], F32)

        def start(reach=None):
            if reach is None:

                @pl.when(to_last > 0)
                def _():
                    message(to_last).start()

            else:

                @pl.when(reach < to_last)
                def _():
                    message(reach).start()

        def carried():
            total = None
            for reach in range(1, n_seq):

                @pl.when(order >= reach)
                def _():
                    message(reach).wait_recv()

            for reach in range(1, n_seq):
                total = dst[reach - 1] if total is None else total + dst[reach - 1]
            return total

        def close():
            for reach in range(1, n_seq):

                @pl.when(reach <= to_last)
                def _():
                    message(reach).wait_send()

        return clear, start, carried, close

    s_clear, s_start, s_carried, s_close = exchange(1, send_s, recv_s, s_send, s_recv)
    t_clear, t_start, t_carried, t_close = exchange(-1, send_t, recv_t, t_send, t_recv)
    s_clear()
    t_clear()
    sums[...] = jnp.zeros_like(sums)

    row = lax.broadcasted_iota(jnp.int32, (block, d), 0)
    token = lax.broadcasted_iota(jnp.int32, (d, block), 1)
    upper = lax.broadcasted_iota(jnp.int32, (block, block), 0) <= lax.broadcasted_iota(jnp.int32, (block, block), 1)

    def take(b):
        return pl.ds(b * block, block)

    def pair(high, low, b):
        return high[take(b), :], low[take(b), :]

    loads[0].wait()
    live = counts[pos] * GROUP

    def keep(source, high, low, b):
        x = jnp.where(row + b * block < live, source[take(b), :], 0.0)
        high[take(b), :], low[take(b), :] = split(x)

    loads[1].wait()
    loads[2].wait()
    before = [jnp.zeros((d, d), F32)]
    for b in range(blocks):
        keep(k_in, k_h, k_l, b)
        keep(v_in, v_h, v_l, b)
        before.append(before[-1] + outer(pair(v_h, v_l, b), pair(k_h, k_l, b)))
    send_s[...] = before[-1]
    pl.semaphore_wait(barrier, n_head - 1 + n_seq - 1)
    s_start()

    loads[3].wait()
    loads[4].wait()
    loads[5].wait()
    scale = head_scale[0]
    gains = gain[...].reshape(1, d)
    for b in range(blocks):
        keep(q_in, q_h, q_l, b)
        q_b, k_b, v_b = pair(q_h, q_l, b), pair(k_h, k_l, b), pair(v_h, v_l, b)
        scores_t = split(jnp.where(upper, rows_by_rows(k_b, q_b), 0.0))
        p_h[take(b), :], p_l[take(b), :] = scores_t
        local = add_rows(dot(beside(v_b), scores_t[0], TN)) + dot(v_b[0], scores_t[1], TN)
        if b:
            local = local + state_by_rows(stacked(split(before[b])), q_b)
        mine_t[:, take(b)] = local
        gg_t[:, take(b)] = jnp.transpose(g_in[take(b), :] * gains)
        for reach in range(1, n_seq - 1):
            if b == min(2 * reach - 2, blocks - 1):
                s_start(reach)

    s_in = s_carried()
    arrived = stacked(split(s_in))
    for b in range(blocks):
        mine = (mine_t[:, take(b)] + state_by_rows(arrived, pair(q_h, q_l, b))) * scale
        mine_t[:, take(b)] = mine
        square = jnp.sum(mine * mine, axis=0, keepdims=True)
        cross = jnp.sum(gg_t[:, take(b)] * mine, axis=0, keepdims=True)
        for j in range(per):
            r = b * per + j
            sums[r : r + 1, :] = square[:, j * GROUP : (j + 1) * GROUP]
            sums[half + r : half + r + 1, :] = cross[:, j * GROUP : (j + 1) * GROUP]

    shares = [
        pltpu.make_async_remote_copy(
            src_ref=sums, dst_ref=sums_in.at[step - 1],
            send_sem=h_send.at[step - 1], recv_sem=h_recv.at[step - 1],
            device_id={"head": lax.rem(head + step, n_head)},
            device_id_type=MESH,
        )
        for step in range(1, n_head)
    ]
    for share in shares:
        share.start()
    total = sums[...]
    for share in shares:
        share.wait_recv()
    for step in range(1, n_head):
        total = total + sums_in[step - 1]
    features = d * n_head
    inverse = lax.rsqrt(total[:half] / features + EPS)
    factor = inverse * inverse * inverse * total[half:] / features

    def along(x, b):
        return jnp.concatenate([x[b * per + j : b * per + j + 1, :] for j in range(per)], axis=1)

    t_states = []
    for b in range(blocks):
        inv, fac = along(inverse, b), along(factor, b)
        grad = (gg_t[:, take(b)] * inv - mine_t[:, take(b)] * fac) * scale
        grad = split(jnp.where(token + b * block < live, grad, 0.0))
        o_h[:, take(b)], o_l[:, take(b)] = grad
        both = dot(jnp.concatenate(grad, axis=0), beside(pair(q_h, q_l, b)), NN)
        t_states.append(add_rows(add_columns(both)))
    after = [jnp.zeros((d, d), F32)]
    for b in range(blocks - 1, -1, -1):
        after.append(after[-1] + t_states[b])
    after = after[::-1]
    send_t[...] = after[0]
    t_start()

    for b in range(blocks):
        q_b, k_b, v_b = pair(q_h, q_l, b), pair(k_h, k_l, b), pair(v_h, v_l, b)
        o_t = o_h[:, take(b)], o_l[:, take(b)]
        o_b = jnp.transpose(o_t[0]), jnp.transpose(o_t[1])
        normed[take(b), :] = jnp.transpose(mine_t[:, take(b)] * along(inverse, b)) * gains
        pulled_t = split(jnp.where(upper, rows_by_columns(v_b, o_t), 0.0))
        gq[take(b), :] = times_state(o_b, split(s_in + before[b])) + columns_times(pulled_t, k_b)
        later = split(after[b + 1])
        gk[take(b), :] = times(pulled_t, q_b) + times_state(v_b, later)
        gv[take(b), :] = times(pair(p_h, p_l, b), o_b) + times_state_t(k_b, later)
        for reach in range(1, n_seq - 1):
            if b == blocks - 1:
                t_start(reach)

    t_out[...] = t_carried()
    s_close()
    for share in shares:
        share.wait_send()
    t_close()


def finish(
    block, normed, gq, gk, gv, k_h, k_l, v_h, v_l, t_in,
    normed_hbm, gq_hbm, gk_hbm, gv_hbm, gk_all, gv_all, sem,
):
    blocks = gk.shape[0] // block
    stores = [
        pltpu.make_async_copy(normed, normed_hbm, sem.at[2 * blocks]),
        pltpu.make_async_copy(gq, gq_hbm, sem.at[2 * blocks + 1]),
    ]
    for store in stores:
        store.start()
    state = split(t_in[...])
    for b in range(blocks):
        rows = pl.ds(b * block, block)
        gk_all[rows, :] = gk[rows, :] + times_state((v_h[rows, :], v_l[rows, :]), state)
        gv_all[rows, :] = gv[rows, :] + times_state_t((k_h[rows, :], k_l[rows, :]), state)
        for i, (src, dst) in enumerate(((gk_all, gk_hbm), (gv_all, gv_hbm))):
            store = pltpu.make_async_copy(src.at[rows, :], dst.at[rows, :], sem.at[2 * b + i])
            store.start()
            stores.append(store)
    for store in stores:
        store.wait()


def on_device(n_seq, n_head, query, key_in, value, out_grad, head_scale, norm_gain, group_counts):
    cap, d = query.shape
    block = 2 * GROUP if cap % (2 * GROUP) == 0 else GROUP
    half = -(-(cap // GROUP) // 8) * 8
    blocks = cap // block
    hbm = pl.BlockSpec(memory_space=pltpu.HBM)
    vmem = pl.BlockSpec(memory_space=pltpu.VMEM)
    wide = pltpu.VMEM((cap, d), F32)
    narrow = pltpu.VMEM((cap, d), BF16)
    state = pltpu.VMEM((d, d), F32)
    states = pltpu.VMEM((n_seq - 1, d, d), F32)
    rows = jax.ShapeDtypeStruct((cap, d), F32)
    rows_low = jax.ShapeDtypeStruct((cap, d), BF16)
    held = pl.pallas_call(
        functools.partial(kernel, n_seq, n_head, block),
        out_shape=[rows] * 4 + [rows_low] * 4 + [jax.ShapeDtypeStruct((d, d), F32)],
        in_specs=[pl.BlockSpec(memory_space=pltpu.SMEM)] + [hbm] * 6,
        out_specs=[vmem] * 9,
        scratch_shapes=[pltpu.SMEM(group_counts.shape, jnp.int32)]
        + [wide] * 4 + [pltpu.VMEM((d,), F32)]
        + [narrow] * 2 + [pltpu.VMEM((cap, block), BF16)] * 2
        + [pltpu.VMEM((d, cap), F32)] * 2 + [pltpu.VMEM((d, cap), BF16)] * 2
        + [state, states] * 2
        + [pltpu.VMEM((2 * half, GROUP), F32), pltpu.VMEM((n_head - 1, 2 * half, GROUP), F32)]
        + [pltpu.SemaphoreType.DMA((6,))]
        + [pltpu.SemaphoreType.DMA((n_seq - 1,))] * 4
        + [pltpu.SemaphoreType.DMA((n_head - 1,))] * 2,
        compiler_params=pltpu.CompilerParams(
            collective_id=0, has_side_effects=True, vmem_limit_bytes=32 * 1024 * 1024
        ),
    )(head_scale, *(
        pltpu.with_memory_space_constraint(x, pltpu.HBM)
        for x in (group_counts, query, key_in, value, out_grad, norm_gain)
    ))
    return pl.pallas_call(
        functools.partial(finish, block),
        out_shape=[rows] * 4,
        in_specs=[vmem] * 9,
        out_specs=[hbm] * 4,
        scratch_shapes=[wide] * 2 + [pltpu.SemaphoreType.DMA((2 * blocks + 2,))],
        compiler_params=pltpu.CompilerParams(vmem_limit_bytes=32 * 1024 * 1024),
    )(*held)


def solution(mesh):
    rows = P("seq", "head")
    return jax.shard_map(
        functools.partial(on_device, mesh.shape["seq"], mesh.shape["head"]),
        mesh=mesh,
        in_specs=(rows, rows, rows, rows, P("head"), P("head"), P()),
        out_specs=(rows, rows, rows, rows),
        check_vma=False,
    )
```

time: 26.3 us -> 24.8 us (0.943)
  the two profiles are of different devices: /device:TPU:0 before, /device:TPU:9 now
where the time goes in v1:
time: 24.8 us; the launch traced here: 24.6 us
  Pallas kernels  23.3 us (94%)
  between operations  1.29 us (5%)
    pallas_call x1, Pallas kernels, on_device(): pl.pallas_call(functools.partial(kernel, n_seq, n_head, block), out_shape...  22.1 us
    pallas_call x1, Pallas kernels, on_device(): pl.pallas_call(functools.partial(finish, block), out_shape=[rows] * 4, in...  1.2 us

profile of v1, /device:TPU:9, one launch (start us, length us, event | category | flops | bytes accessed | tf_op | source)
XLA Modules:
  0.0 24.6 jit_solution(124972414724382724)
XLA Ops:
  1.3 22.1 %shard_map.102 = (f32[768,128]{1,0:T(8,128)S(1)}, f32[768,128]{1,0:T(8,128)S(1)}, f32[768,128]{1,0:T(8,128)S(1)}, f32[768,128]{1,0:T(8,128)S(1)}, bf16[768,128]{...) custom-call(f32[1]{0:T(128)S(6)} %copy.11.head_scale, ...), custom_call_target="tpu_custom_call" | custom-call | tf_op jit(solution)/shard_map/pallas_call | solution.py:334
  23.4 1.2 %shard_map.103 = (f32[768,128]{1,0:T(8,128)}, f32[768,128]{1,0:T(8,128)}, f32[768,128]{1,0:T(8,128)}, f32[768,128]{1,0:T(8,128)}) custom-call(f32[768,128]{1,0:T(8,128)S(1)} %get-tuple-element.13.normed, f32[768,128]{1,0:T(8,128)S(1)} %get-tuple-element.14.gq, f32[768,128]{1,0:T(8,128)S(1)} %get-tuple-element.15.gk, f32[768,128]{1,0:T(8,128)S(1)} %get-tuple-element.16.gv, ...), custom_call_target="tpu_custom_call" | custom-call | tf_op jit(solution)/shard_map/pallas_call | solution.py:355

commit v2 on v1

--- a/solution.py
+++ b/solution.py
@@ -8,6 +8,7 @@
 from jax.sharding import PartitionSpec as P
 
 GROUP = 128
+CHUNKS = 4
 EPS = 1e-05
 F32 = jnp.float32
 BF16 = jnp.bfloat16
@@ -91,8 +92,8 @@
     normed, gq, gk, gv, k_h, k_l, v_h, v_l, t_out,
     counts, q_in, k_in, v_in, g_in, gain,
     q_h, q_l, p_h, p_l, mine_t, gg_t, o_h, o_l,
-    send_s, recv_s, send_t, recv_t, sums, sums_in,
-    in_sem, s_send, s_recv, t_send, t_recv, h_send, h_recv,
+    send_s, pass_s, near_s, far_s, send_t, pass_t, near_t, far_t, sums, sums_in,
+    in_sem, h_send, h_recv, *seq_sems,
 ):
     cap, d = q_in.shape
     blocks = cap // block
@@ -100,6 +101,8 @@
     pos = lax.axis_index("seq")
     head = lax.axis_index("head")
     half = sums.shape[0] // 2
+
+    s_sems, t_sems = seq_sems[:4], seq_sems[4:]
 
     barrier = pltpu.get_barrier_semaphore()
     for step in range(1, n_seq):
@@ -118,63 +121,110 @@
     for step in range(1, n_head):
         pl.semaphore_signal(barrier, inc=1, device_id={"head": lax.rem(head + step, n_head)}, device_id_type=MESH)
 
-    def exchange(way, src, dst, s_sem, r_sem):
+    def exchange(way, src, passed, near, far, sems):
+        far_send, far_recv, near_send, near_recv = sems
         order = pos if way == 1 else n_seq - 1 - pos
-        to_last = n_seq - 1 - order
-
-        def message(reach):
+        last = n_seq - 1
+        direct = n_seq <= 4
+        middle = jnp.logical_and(order > 0, order < (last - 1 if direct else last))
+        heads_chain = jnp.logical_and(order == 0, last > (1 if direct else 0))
+
+        def to_last():
             return pltpu.make_async_remote_copy(
-                src_ref=src, dst_ref=dst.at[reach - 1],
-                send_sem=s_sem.at[reach - 1], recv_sem=r_sem.at[reach - 1],
-                device_id={"seq": pos + way * reach}, device_id_type=MESH,
+                src_ref=src, dst_ref=far.at[order], send_sem=far_send, recv_sem=far_recv.at[order],
+                device_id={"seq": last if way == 1 else 0}, device_id_type=MESH,
             )
 
+        def from_order(k):
+            return pltpu.make_async_remote_copy(
+                src_ref=src, dst_ref=far.at[k], send_sem=far_send, recv_sem=far_recv.at[k],
+                device_id={"seq": last if way == 1 else 0}, device_id_type=MESH,
+            )
+
+        def to_next(source, c):
+            rows = pl.ds(c * (d // CHUNKS), d // CHUNKS)
+            return pltpu.make_async_remote_copy(
+                src_ref=source.at[rows, :], dst_ref=near.at[rows, :],
+                send_sem=near_send.at[c], recv_sem=near_recv.at[c],
+                device_id={"seq": pos + way}, device_id_type=MESH,
+            )
+
         def clear():
-            for reach in range(1, n_seq):
-
-                @pl.when(order < reach)
+            @pl.when(jnp.logical_or(order == 0, order == last) if direct else order == 0)
+            def _():
+                near[...] = jnp.zeros_like(near)
+
+            if direct:
+
+                @pl.when(order < last)
                 def _():
-                    dst[reach - 1] = jnp.zeros(dst.shape[1:], F32)
-
-        def start(reach=None):
-            if reach is None:
-
-                @pl.when(to_last > 0)
+                    far[...] = jnp.zeros_like(far)
+
+        def start():
+            if direct:
+
+                @pl.when(order < last)
                 def _():
-                    message(to_last).start()
+                    to_last().start()
+
+            @pl.when(heads_chain)
+            def _():
+                for c in range(CHUNKS):
+                    to_next(src, c).start()
+
+        def carried():
+            @pl.when(middle)
+            def _():
+                for c in range(CHUNKS):
+                    rows = pl.ds(c * (d // CHUNKS), d // CHUNKS)
+                    to_next(src, c).wait_recv()
+                    passed[rows, :] = src[rows, :] + near[rows, :]
+                    to_next(passed, c).start()
+
+            if direct:
+                if last > 1:
+
+                    @pl.when(order == last - 1)
+                    def _():
+                        for c in range(CHUNKS):
+                            to_next(src, c).wait_recv()
+
+                @pl.when(order == last)
+                def _():
+                    for k in range(last):
+                        from_order(k).wait_recv()
 
             else:
 
-                @pl.when(reach < to_last)
+                @pl.when(order == last)
                 def _():
-                    message(reach).start()
-
-        def carried():
-            total = None
-            for reach in range(1, n_seq):
-
-                @pl.when(order >= reach)
+                    for c in range(CHUNKS):
+                        to_next(src, c).wait_recv()
+
+            total = near[...]
+            if direct:
+                for k in range(last):
+                    total = total + far[k]
+            return total
+
+        def close():
+            if direct:
+
+                @pl.when(order < last)
                 def _():
-                    message(reach).wait_recv()
-
-            for reach in range(1, n_seq):
-                total = dst[reach - 1] if total is None else total + dst[reach - 1]
-            return total
-
-        def close():
-            for reach in range(1, n_seq):
-
-                @pl.when(reach <= to_last)
-                def _():
-                    message(reach).wait_send()
+                    to_last().wait_send()
+
+            @pl.when(jnp.logical_or(heads_chain, middle))
+            def _():
+                for c in range(CHUNKS):
+                    to_next(src, c).wait_send()
 
         return clear, start, carried, close
 
-    s_clear, s_start, s_carried, s_close = exchange(1, send_s, recv_s, s_send, s_recv)
-    t_clear, t_start, t_carried, t_close = exchange(-1, send_t, recv_t, t_send, t_recv)
+    s_clear, s_start, s_carried, s_close = exchange(1, send_s, pass_s, near_s, far_s, s_sems)
+    t_clear, t_start, t_carried, t_close = exchange(-1, send_t, pass_t, near_t, far_t, t_sems)
     s_clear()
     t_clear()
-    sums[...] = jnp.zeros_like(sums)
 
     row = lax.broadcasted_iota(jnp.int32, (block, d), 0)
     token = lax.broadcasted_iota(jnp.int32, (d, block), 1)
@@ -219,9 +269,6 @@
             local = local + state_by_rows(stacked(split(before[b])), q_b)
         mine_t[:, take(b)] = local
         gg_t[:, take(b)] = jnp.transpose(g_in[take(b), :] * gains)
-        for reach in range(1, n_seq - 1):
-            if b == min(2 * reach - 2, blocks - 1):
-                s_start(reach)
 
     s_in = s_carried()
     arrived = stacked(split(s_in))
@@ -235,14 +282,23 @@
             sums[r : r + 1, :] = square[:, j * GROUP : (j + 1) * GROUP]
             sums[half + r : half + r + 1, :] = cross[:, j * GROUP : (j + 1) * GROUP]
 
+    def partner(step):
+        if n_head & (n_head - 1):
+            return lax.rem(head + step, n_head)
+        other, bit = head, 1
+        while bit < n_head:
+            if step & bit:
+                other = other + bit - 2 * bit * lax.rem(head // bit, 2)
+            bit *= 2
+        return other
+
     shares = [
         pltpu.make_async_remote_copy(
             src_ref=sums, dst_ref=sums_in.at[step - 1],
             send_sem=h_send.at[step - 1], recv_sem=h_recv.at[step - 1],
-            device_id={"head": lax.rem(head + step, n_head)},
-            device_id_type=MESH,
+            device_id={"head": partner(step)}, device_id_type=MESH,
         )
-        for step in range(1, n_head)
+        for step in range(n_head - 1, 0, -1)
     ]
     for share in shares:
         share.start()
@@ -283,14 +339,11 @@
         later = split(after[b + 1])
         gk[take(b), :] = times(pulled_t, q_b) + times_state(v_b, later)
         gv[take(b), :] = times(pair(p_h, p_l, b), o_b) + times_state_t(k_b, later)
-        for reach in range(1, n_seq - 1):
-            if b == blocks - 1:
-                t_start(reach)
-
-    t_out[...] = t_carried()
+
     s_close()
     for share in shares:
         share.wait_send()
+    t_out[...] = t_carried()
     t_close()
 
 
@@ -321,7 +374,7 @@
 def on_device(n_seq, n_head, query, key_in, value, out_grad, head_scale, norm_gain, group_counts):
     cap, d = query.shape
     block = 2 * GROUP if cap % (2 * GROUP) == 0 else GROUP
-    half = -(-(cap // GROUP) // 8) * 8
+    half = cap // GROUP
     blocks = cap // block
     hbm = pl.BlockSpec(memory_space=pltpu.HBM)
     vmem = pl.BlockSpec(memory_space=pltpu.VMEM)
@@ -340,11 +393,14 @@
         + [wide] * 4 + [pltpu.VMEM((d,), F32)]
         + [narrow] * 2 + [pltpu.VMEM((cap, block), BF16)] * 2
         + [pltpu.VMEM((d, cap), F32)] * 2 + [pltpu.VMEM((d, cap), BF16)] * 2
-        + [state, states] * 2
+        + [state, state, state, states] * 2
         + [pltpu.VMEM((2 * half, GROUP), F32), pltpu.VMEM((n_head - 1, 2 * half, GROUP), F32)]
         + [pltpu.SemaphoreType.DMA((6,))]
-        + [pltpu.SemaphoreType.DMA((n_seq - 1,))] * 4
-        + [pltpu.SemaphoreType.DMA((n_head - 1,))] * 2,
+        + [pltpu.SemaphoreType.DMA((n_head - 1,))] * 2
+        + [
+            pltpu.SemaphoreType.DMA, pltpu.SemaphoreType.DMA((n_seq - 1,)),
+            pltpu.SemaphoreType.DMA((CHUNKS,)), pltpu.SemaphoreType.DMA((CHUNKS,)),
+        ] * 2,
         compiler_params=pltpu.CompilerParams(
             collective_id=0, has_side_effects=True, vmem_limit_bytes=32 * 1024 * 1024
         ),

time: 24.8 us -> 23.8 us (0.960)
  the two profiles are of different devices: /device:TPU:9 before, /device:TPU:0 now
where the time goes in v2:
time: 23.8 us; the launch traced here: 23.7 us
  Pallas kernels  22.4 us (94%)
  between operations  1.29 us (5%)
    pallas_call x1, Pallas kernels, on_device(): pl.pallas_call(functools.partial(kernel, n_seq, n_head, block), out_shape...  21.2 us
    pallas_call x1, Pallas kernels, on_device(): pl.pallas_call(functools.partial(finish, block), out_shape=[rows] * 4, in...  1.2 us

profile of v2, /device:TPU:0, one launch (start us, length us, event | category | flops | bytes accessed | tf_op | source)
XLA Modules:
  0.0 23.7 jit_solution(2412469222765831619)
XLA Ops:
  1.3 21.2 %shard_map.102 = (f32[768,128]{1,0:T(8,128)S(1)}, f32[768,128]{1,0:T(8,128)S(1)}, f32[768,128]{1,0:T(8,128)S(1)}, f32[768,128]{1,0:T(8,128)S(1)}, bf16[768,128]{...) custom-call(f32[1]{0:T(128)S(6)} %copy.11.head_scale, ...), custom_call_target="tpu_custom_call" | custom-call | tf_op jit(solution)/shard_map/pallas_call | solution.py:387
  22.5 1.2 %shard_map.103 = (f32[768,128]{1,0:T(8,128)}, f32[768,128]{1,0:T(8,128)}, f32[768,128]{1,0:T(8,128)}, f32[768,128]{1,0:T(8,128)}) custom-call(f32[768,128]{1,0:T(8,128)S(1)} %get-tuple-element.13.normed, f32[768,128]{1,0:T(8,128)S(1)} %get-tuple-element.14.gq, f32[768,128]{1,0:T(8,128)S(1)} %get-tuple-element.15.gk, f32[768,128]{1,0:T(8,128)S(1)} %get-tuple-element.16.gv, ...), custom_call_target="tpu_custom_call" | custom-call | tf_op jit(solution)/shard_map/pallas_call | solution.py:411

commit v3 on v2

--- a/solution.py
+++ b/solution.py
@@ -9,6 +9,7 @@
 
 GROUP = 128
 CHUNKS = 4
+PARTS = 2
 EPS = 1e-05
 F32 = jnp.float32
 BF16 = jnp.bfloat16
@@ -129,20 +130,18 @@
         middle = jnp.logical_and(order > 0, order < (last - 1 if direct else last))
         heads_chain = jnp.logical_and(order == 0, last > (1 if direct else 0))
 
-        def to_last():
+        def piece(p, parts):
+            return pl.ds(p * (d // parts), d // parts)
+
+        def far_copy(k, p):
             return pltpu.make_async_remote_copy(
-                src_ref=src, dst_ref=far.at[order], send_sem=far_send, recv_sem=far_recv.at[order],
+                src_ref=src.at[piece(p, PARTS), :], dst_ref=far.at[k, piece(p, PARTS), :],
+                send_sem=far_send.at[p], recv_sem=far_recv.at[k, p],
                 device_id={"seq": last if way == 1 else 0}, device_id_type=MESH,
             )
 
-        def from_order(k):
-            return pltpu.make_async_remote_copy(
-                src_ref=src, dst_ref=far.at[k], send_sem=far_send, recv_sem=far_recv.at[k],
-                device_id={"seq": last if way == 1 else 0}, device_id_type=MESH,
-            )
-
         def to_next(source, c):
-            rows = pl.ds(c * (d // CHUNKS), d // CHUNKS)
+            rows = piece(c, CHUNKS)
             return pltpu.make_async_remote_copy(
                 src_ref=source.at[rows, :], dst_ref=near.at[rows, :],
                 send_sem=near_send.at[c], recv_sem=near_recv.at[c],
@@ -160,51 +159,48 @@
                 def _():
                     far[...] = jnp.zeros_like(far)
 
-        def start():
+        def start_last(p):
             if direct:
 
                 @pl.when(order < last)
                 def _():
-                    to_last().start()
-
+                    far_copy(order, p).start()
+
+        def start_next():
             @pl.when(heads_chain)
             def _():
                 for c in range(CHUNKS):
                     to_next(src, c).start()
 
-        def carried():
+        def carried(p):
+            per_part = CHUNKS // PARTS
+
             @pl.when(middle)
             def _():
-                for c in range(CHUNKS):
-                    rows = pl.ds(c * (d // CHUNKS), d // CHUNKS)
+                for c in range(p * per_part, (p + 1) * per_part):
+                    rows = piece(c, CHUNKS)
                     to_next(src, c).wait_recv()
                     passed[rows, :] = src[rows, :] + near[rows, :]
                     to_next(passed, c).start()
 
+            if not direct or last > 1:
+
+                @pl.when(order == (last - 1 if direct else last))
+                def _():
+                    for c in range(p * per_part, (p + 1) * per_part):
+                        to_next(src, c).wait_recv()
+
             if direct:
-                if last > 1:
-
-                    @pl.when(order == last - 1)
-                    def _():
-                        for c in range(CHUNKS):
-                            to_next(src, c).wait_recv()
 
                 @pl.when(order == last)
                 def _():
                     for k in range(last):
-                        from_order(k).wait_recv()
-
-            else:
-
-                @pl.when(order == last)
-                def _():
-                    for c in range(CHUNKS):
-                        to_next(src, c).wait_recv()
-
-            total = near[...]
+                        far_copy(k, p).wait_recv()
+
+            total = near[piece(p, PARTS), :]
             if direct:
                 for k in range(last):
-                    total = total + far[k]
+                    total = total + far[k, piece(p, PARTS), :]
             return total
 
         def close():
@@ -212,22 +208,22 @@
 
                 @pl.when(order < last)
                 def _():
-                    to_last().wait_send()
+                    for p in range(PARTS):
+                        far_copy(order, p).wait_send()
 
             @pl.when(jnp.logical_or(heads_chain, middle))
             def _():
                 for c in range(CHUNKS):
                     to_next(src, c).wait_send()
 
-        return clear, start, carried, close
-
-    s_clear, s_start, s_carried, s_close = exchange(1, send_s, pass_s, near_s, far_s, s_sems)
-    t_clear, t_start, t_carried, t_close = exchange(-1, send_t, pass_t, near_t, far_t, t_sems)
+        return clear, start_last, start_next, carried, close
+
+    s_clear, s_last, s_next, s_carried, s_close = exchange(1, send_s, pass_s, near_s, far_s, s_sems)
+    t_clear, t_last, t_next, t_carried, t_close = exchange(-1, send_t, pass_t, near_t, far_t, t_sems)
     s_clear()
     t_clear()
 
     row = lax.broadcasted_iota(jnp.int32, (block, d), 0)
-    token = lax.broadcasted_iota(jnp.int32, (d, block), 1)
     upper = lax.broadcasted_iota(jnp.int32, (block, block), 0) <= lax.broadcasted_iota(jnp.int32, (block, block), 1)
 
     def take(b):
@@ -252,7 +248,9 @@
         before.append(before[-1] + outer(pair(v_h, v_l, b), pair(k_h, k_l, b)))
     send_s[...] = before[-1]
     pl.semaphore_wait(barrier, n_head - 1 + n_seq - 1)
-    s_start()
+    s_next()
+    for p in range(PARTS):
+        s_last(p)
 
     loads[3].wait()
     loads[4].wait()
@@ -270,17 +268,25 @@
         mine_t[:, take(b)] = local
         gg_t[:, take(b)] = jnp.transpose(g_in[take(b), :] * gains)
 
-    s_in = s_carried()
-    arrived = stacked(split(s_in))
-    for b in range(blocks):
-        mine = (mine_t[:, take(b)] + state_by_rows(arrived, pair(q_h, q_l, b))) * scale
-        mine_t[:, take(b)] = mine
-        square = jnp.sum(mine * mine, axis=0, keepdims=True)
-        cross = jnp.sum(gg_t[:, take(b)] * mine, axis=0, keepdims=True)
+    s_parts = []
+    square, cross = [None] * blocks, [None] * blocks
+    for p in range(PARTS):
+        rows = pl.ds(p * (d // PARTS), d // PARTS)
+        s_parts.append(s_carried(p))
+        arrived = stacked(split(s_parts[p]))
+        for b in range(blocks):
+            mine = (mine_t[rows, take(b)] + state_by_rows(arrived, pair(q_h, q_l, b))) * scale
+            mine_t[rows, take(b)] = mine
+            squares = jnp.sum(mine * mine, axis=0, keepdims=True)
+            crosses = jnp.sum(gg_t[rows, take(b)] * mine, axis=0, keepdims=True)
+            square[b] = square[b] + squares if p else squares
+            cross[b] = cross[b] + crosses if p else crosses
+    s_in = jnp.concatenate(s_parts, axis=0)
+    for b in range(blocks):
         for j in range(per):
             r = b * per + j
-            sums[r : r + 1, :] = square[:, j * GROUP : (j + 1) * GROUP]
-            sums[half + r : half + r + 1, :] = cross[:, j * GROUP : (j + 1) * GROUP]
+            sums[r : r + 1, :] = square[b][:, j * GROUP : (j + 1) * GROUP]
+            sums[half + r : half + r + 1, :] = cross[b][:, j * GROUP : (j + 1) * GROUP]
 
     def partner(step):
         if n_head & (n_head - 1):
@@ -314,20 +320,27 @@
     def along(x, b):
         return jnp.concatenate([x[b * per + j : b * per + j + 1, :] for j in range(per)], axis=1)
 
-    t_states = []
-    for b in range(blocks):
-        inv, fac = along(inverse, b), along(factor, b)
-        grad = (gg_t[:, take(b)] * inv - mine_t[:, take(b)] * fac) * scale
-        grad = split(jnp.where(token + b * block < live, grad, 0.0))
-        o_h[:, take(b)], o_l[:, take(b)] = grad
-        both = dot(jnp.concatenate(grad, axis=0), beside(pair(q_h, q_l, b)), NN)
-        t_states.append(add_rows(add_columns(both)))
+    t_parts = [[] for _ in range(blocks)]
+    for p in range(PARTS):
+        rows = pl.ds(p * (d // PARTS), d // PARTS)
+        token = lax.broadcasted_iota(jnp.int32, (d // PARTS, block), 1)
+        whole = None
+        for b in range(blocks):
+            inv, fac = along(inverse, b), along(factor, b)
+            grad = (gg_t[rows, take(b)] * inv - mine_t[rows, take(b)] * fac) * scale
+            grad = split(jnp.where(token + b * block < live, grad, 0.0))
+            o_h[rows, take(b)], o_l[rows, take(b)] = grad
+            both = dot(jnp.concatenate(grad, axis=0), beside(pair(q_h, q_l, b)), NN)
+            t_parts[b].append(add_rows(add_columns(both)))
+            whole = t_parts[b][p] if whole is None else whole + t_parts[b][p]
+        send_t[rows, :] = whole
+        t_last(p)
+    t_next()
+    t_states = [jnp.concatenate(parts, axis=0) for parts in t_parts]
     after = [jnp.zeros((d, d), F32)]
     for b in range(blocks - 1, -1, -1):
         after.append(after[-1] + t_states[b])
     after = after[::-1]
-    send_t[...] = after[0]
-    t_start()
 
     for b in range(blocks):
         q_b, k_b, v_b = pair(q_h, q_l, b), pair(k_h, k_l, b), pair(v_h, v_l, b)
@@ -343,7 +356,8 @@
     s_close()
     for share in shares:
         share.wait_send()
-    t_out[...] = t_carried()
+    for p in range(PARTS):
+        t_out[pl.ds(p * (d // PARTS), d // PARTS), :] = t_carried(p)
     t_close()
 
 
@@ -359,14 +373,21 @@
     for store in stores:
         store.start()
     state = split(t_in[...])
+
+    def save(src, dst, b, i):
+        rows = pl.ds(b * block, block)
+        store = pltpu.make_async_copy(src.at[rows, :], dst.at[rows, :], sem.at[2 * b + i])
+        store.start()
+        stores.append(store)
+
     for b in range(blocks):
         rows = pl.ds(b * block, block)
         gk_all[rows, :] = gk[rows, :] + times_state((v_h[rows, :], v_l[rows, :]), state)
+        save(gk_all, gk_hbm, b, 0)
+    for b in range(blocks):
+        rows = pl.ds(b * block, block)
         gv_all[rows, :] = gv[rows, :] + times_state_t((k_h[rows, :], k_l[rows, :]), state)
-        for i, (src, dst) in enumerate(((gk_all, gk_hbm), (gv_all, gv_hbm))):
-            store = pltpu.make_async_copy(src.at[rows, :], dst.at[rows, :], sem.at[2 * b + i])
-            store.start()
-            stores.append(store)
+        save(gv_all, gv_hbm, b, 1)
     for store in stores:
         store.wait()
 
@@ -398,7 +419,7 @@
         + [pltpu.SemaphoreType.DMA((6,))]
         + [pltpu.SemaphoreType.DMA((n_head - 1,))] * 2
         + [
-            pltpu.SemaphoreType.DMA, pltpu.SemaphoreType.DMA((n_seq - 1,)),
+            pltpu.SemaphoreType.DMA((PARTS,)), pltpu.SemaphoreType.DMA((n_seq - 1, PARTS)),
             pltpu.SemaphoreType.DMA((CHUNKS,)), pltpu.SemaphoreType.DMA((CHUNKS,)),
         ] * 2,
         compiler_params=pltpu.CompilerParams(

time: 23.8 us -> 23.7 us (level)
  no operation moved by 1% of the time
where the time goes in v3:
time: 23.7 us; the launch traced here: 23.6 us
  Pallas kernels  22.3 us (94%)
  between operations  1.29 us (5%)
    pallas_call x1, Pallas kernels, on_device(): pl.pallas_call(functools.partial(kernel, n_seq, n_head, block), out_shape...  21.1 us
    pallas_call x1, Pallas kernels, on_device(): pl.pallas_call(functools.partial(finish, block), out_shape=[rows] * 4, in...  1.2 us

profile of v3, /device:TPU:0, one launch (start us, length us, event | category | flops | bytes accessed | tf_op | source)
XLA Modules:
  0.0 23.6 jit_solution(12730870908417191465)
XLA Ops:
  1.3 21.1 %shard_map.102 = (f32[768,128]{1,0:T(8,128)S(1)}, f32[768,128]{1,0:T(8,128)S(1)}, f32[768,128]{1,0:T(8,128)S(1)}, f32[768,128]{1,0:T(8,128)S(1)}, bf16[768,128]{...) custom-call(f32[1]{0:T(128)S(6)} %copy.11.head_scale, ...), custom_call_target="tpu_custom_call" | custom-call | tf_op jit(solution)/shard_map/pallas_call | solution.py:408
  22.4 1.2 %shard_map.103 = (f32[768,128]{1,0:T(8,128)}, f32[768,128]{1,0:T(8,128)}, f32[768,128]{1,0:T(8,128)}, f32[768,128]{1,0:T(8,128)}) custom-call(f32[768,128]{1,0:T(8,128)S(1)} %get-tuple-element.13.normed, f32[768,128]{1,0:T(8,128)S(1)} %get-tuple-element.14.gq, f32[768,128]{1,0:T(8,128)S(1)} %get-tuple-element.15.gk, f32[768,128]{1,0:T(8,128)S(1)} %get-tuple-element.16.gv, ...), custom_call_target="tpu_custom_call" | custom-call | tf_op jit(solution)/shard_map/pallas_call | solution.py:432

commit v4 on v3

--- a/solution.py
+++ b/solution.py
@@ -102,6 +102,7 @@
     pos = lax.axis_index("seq")
     head = lax.axis_index("head")
     half = sums.shape[0] // 2
+    second = lax.rem(head, 2) == 1
 
     s_sems, t_sems = seq_sems[:4], seq_sems[4:]
 
@@ -130,12 +131,15 @@
         middle = jnp.logical_and(order > 0, order < (last - 1 if direct else last))
         heads_chain = jnp.logical_and(order == 0, last > (1 if direct else 0))
 
+        merge = way == -1 and direct and last == 3
+        merged = jnp.logical_and(second, order <= 1) if merge else False
+
         def piece(p, parts):
             return pl.ds(p * (d // parts), d // parts)
 
-        def far_copy(k, p):
+        def far_copy(k, p, source=src):
             return pltpu.make_async_remote_copy(
-                src_ref=src.at[piece(p, PARTS), :], dst_ref=far.at[k, piece(p, PARTS), :],
+                src_ref=source.at[piece(p, PARTS), :], dst_ref=far.at[k, piece(p, PARTS), :],
                 send_sem=far_send.at[p], recv_sem=far_recv.at[k, p],
                 device_id={"seq": last if way == 1 else 0}, device_id_type=MESH,
             )
@@ -159,10 +163,16 @@
                 def _():
                     far[...] = jnp.zeros_like(far)
 
+                if merge:
+
+                    @pl.when(jnp.logical_and(order == last, second))
+                    def _():
+                        far[0] = jnp.zeros(far.shape[1:], F32)
+
         def start_last(p):
             if direct:
 
-                @pl.when(order < last)
+                @pl.when(jnp.logical_and(order < last, jnp.logical_not(merged)))
                 def _():
                     far_copy(order, p).start()
 
@@ -172,16 +182,38 @@
                 for c in range(CHUNKS):
                     to_next(src, c).start()
 
-        def carried(p):
-            per_part = CHUNKS // PARTS
-
-            @pl.when(middle)
+        def relay(p, when):
+            chunks = range(p * (CHUNKS // PARTS), (p + 1) * (CHUNKS // PARTS))
+
+            def pass_on():
+                for c in chunks:
+                    to_next(passed, c).start()
+
+            @pl.when(jnp.logical_and(middle, when))
             def _():
-                for c in range(p * per_part, (p + 1) * per_part):
+                for c in chunks:
                     rows = piece(c, CHUNKS)
                     to_next(src, c).wait_recv()
                     passed[rows, :] = src[rows, :] + near[rows, :]
-                    to_next(passed, c).start()
+                    if not merge:
+                        to_next(passed, c).start()
+
+                if merge:
+
+                    @pl.when(merged)
+                    def _():
+                        far_copy(1, p, passed).start()
+
+                        if p == PARTS - 1:
+                            for c in range(CHUNKS):
+                                to_next(passed, c).start()
+
+                    @pl.when(jnp.logical_not(merged))
+                    def _():
+                        pass_on()
+
+        def carried(p):
+            per_part = CHUNKS // PARTS
 
             if not direct or last > 1:
 
@@ -194,8 +226,14 @@
 
                 @pl.when(order == last)
                 def _():
-                    for k in range(last):
+                    for k in range(1 if merge else 0, last):
                         far_copy(k, p).wait_recv()
+
+                if merge:
+
+                    @pl.when(jnp.logical_and(order == last, jnp.logical_not(second)))
+                    def _():
+                        far_copy(0, p).wait_recv()
 
             total = near[piece(p, PARTS), :]
             if direct:
@@ -206,7 +244,7 @@
         def close():
             if direct:
 
-                @pl.when(order < last)
+                @pl.when(jnp.logical_and(order < last, jnp.logical_or(order > 0, jnp.logical_not(merged))))
                 def _():
                     for p in range(PARTS):
                         far_copy(order, p).wait_send()
@@ -216,10 +254,10 @@
                 for c in range(CHUNKS):
                     to_next(src, c).wait_send()
 
-        return clear, start_last, start_next, carried, close
-
-    s_clear, s_last, s_next, s_carried, s_close = exchange(1, send_s, pass_s, near_s, far_s, s_sems)
-    t_clear, t_last, t_next, t_carried, t_close = exchange(-1, send_t, pass_t, near_t, far_t, t_sems)
+        return clear, start_last, start_next, relay, carried, close
+
+    s_clear, s_last, s_next, s_relay, s_carried, s_close = exchange(1, send_s, pass_s, near_s, far_s, s_sems)
+    t_clear, t_last, t_next, t_relay, t_carried, t_close = exchange(-1, send_t, pass_t, near_t, far_t, t_sems)
     s_clear()
     t_clear()
 
@@ -272,6 +310,7 @@
     square, cross = [None] * blocks, [None] * blocks
     for p in range(PARTS):
         rows = pl.ds(p * (d // PARTS), d // PARTS)
+        s_relay(p, True)
         s_parts.append(s_carried(p))
         arrived = stacked(split(s_parts[p]))
         for b in range(blocks):
@@ -352,11 +391,15 @@
         later = split(after[b + 1])
         gk[take(b), :] = times(pulled_t, q_b) + times_state(v_b, later)
         gv[take(b), :] = times(pair(p_h, p_l, b), o_b) + times_state_t(k_b, later)
+        if b == 1:
+            for p in range(PARTS):
+                t_relay(p, second)
 
     s_close()
     for share in shares:
         share.wait_send()
     for p in range(PARTS):
+        t_relay(p, jnp.logical_not(second))
         t_out[pl.ds(p * (d // PARTS), d // PARTS), :] = t_carried(p)
     t_close()
 

time: 23.7 us -> 23.5 us (level)
  Pallas kernels: 22.3 us -> 22 us
    pallas_call x1, Pallas kernels: 21.1 us -> 20.8 us  [on_device(): pl.pallas_call(functools.partial(kernel, n_seq, n_head, block), out_shape...]
where the time goes in v4:
time: 23.5 us; the launch traced here: 23.3 us
  Pallas kernels  22 us (94%)
  between operations  1.29 us (5%)
    pallas_call x1, Pallas kernels, on_device(): pl.pallas_call(functools.partial(kernel, n_seq, n_head, block), out_shape...  20.8 us
    pallas_call x1, Pallas kernels, on_device(): pl.pallas_call(functools.partial(finish, block), out_shape=[rows] * 4, in...  1.2 us

profile of v4, /device:TPU:0, one launch (start us, length us, event | category | flops | bytes accessed | tf_op | source)
XLA Modules:
  0.0 23.3 jit_solution(15003580390367689802)
XLA Ops:
  1.3 20.8 %shard_map.102 = (f32[768,128]{1,0:T(8,128)S(1)}, f32[768,128]{1,0:T(8,128)S(1)}, f32[768,128]{1,0:T(8,128)S(1)}, f32[768,128]{1,0:T(8,128)S(1)}, bf16[768,128]{...) custom-call(f32[1]{0:T(128)S(6)} %copy.11.head_scale, ...), custom_call_target="tpu_custom_call" | custom-call | tf_op jit(solution)/shard_map/pallas_call | solution.py:451
  22.1 1.2 %shard_map.103 = (f32[768,128]{1,0:T(8,128)}, f32[768,128]{1,0:T(8,128)}, f32[768,128]{1,0:T(8,128)}, f32[768,128]{1,0:T(8,128)}) custom-call(f32[768,128]{1,0:T(8,128)S(1)} %get-tuple-element.13.normed, f32[768,128]{1,0:T(8,128)S(1)} %get-tuple-element.14.gq, f32[768,128]{1,0:T(8,128)S(1)} %get-tuple-element.15.gk, f32[768,128]{1,0:T(8,128)S(1)} %get-tuple-element.16.gv, ...), custom_call_target="tpu_custom_call" | custom-call | tf_op jit(solution)/shard_map/pallas_call | solution.py:475

commit v5 on v4

--- a/solution.py
+++ b/solution.py
@@ -8,7 +8,7 @@
 from jax.sharding import PartitionSpec as P
 
 GROUP = 128
-CHUNKS = 4
+CHUNKS = 2
 PARTS = 2
 EPS = 1e-05
 F32 = jnp.float32
@@ -131,7 +131,7 @@
         middle = jnp.logical_and(order > 0, order < (last - 1 if direct else last))
         heads_chain = jnp.logical_and(order == 0, last > (1 if direct else 0))
 
-        merge = way == -1 and direct and last == 3
+        merge = direct and last == 3
         merged = jnp.logical_and(second, order <= 1) if merge else False
 
         def piece(p, parts):
@@ -306,11 +306,12 @@
         mine_t[:, take(b)] = local
         gg_t[:, take(b)] = jnp.transpose(g_in[take(b), :] * gains)
 
+    for p in range(PARTS):
+        s_relay(p, True)
     s_parts = []
     square, cross = [None] * blocks, [None] * blocks
     for p in range(PARTS):
         rows = pl.ds(p * (d // PARTS), d // PARTS)
-        s_relay(p, True)
         s_parts.append(s_carried(p))
         arrived = stacked(split(s_parts[p]))
         for b in range(blocks):

time: 23.5 us -> 23.2 us (0.987)
  no operation moved by 1% of the time
where the time goes in v5:
time: 23.2 us; the launch traced here: 23 us
  Pallas kernels  21.8 us (94%)
  between operations  1.29 us (6%)
    pallas_call x1, Pallas kernels, on_device(): pl.pallas_call(functools.partial(kernel, n_seq, n_head, block), out_shape...  20.6 us
    pallas_call x1, Pallas kernels, on_device(): pl.pallas_call(functools.partial(finish, block), out_shape=[rows] * 4, in...  1.2 us

profile of v5, /device:TPU:0, one launch (start us, length us, event | category | flops | bytes accessed | tf_op | source)
XLA Modules:
  0.0 23.0 jit_solution(17585529939127552243)
XLA Ops:
  1.3 20.6 %shard_map.102 = (f32[768,128]{1,0:T(8,128)S(1)}, f32[768,128]{1,0:T(8,128)S(1)}, f32[768,128]{1,0:T(8,128)S(1)}, f32[768,128]{1,0:T(8,128)S(1)}, bf16[768,128]{...) custom-call(f32[1]{0:T(128)S(6)} %copy.11.head_scale, ...), custom_call_target="tpu_custom_call" | custom-call | tf_op jit(solution)/shard_map/pallas_call | solution.py:452
  21.8 1.2 %shard_map.103 = (f32[768,128]{1,0:T(8,128)}, f32[768,128]{1,0:T(8,128)}, f32[768,128]{1,0:T(8,128)}, f32[768,128]{1,0:T(8,128)}) custom-call(f32[768,128]{1,0:T(8,128)S(1)} %get-tuple-element.13.normed, f32[768,128]{1,0:T(8,128)S(1)} %get-tuple-element.14.gq, f32[768,128]{1,0:T(8,128)S(1)} %get-tuple-element.15.gk, f32[768,128]{1,0:T(8,128)S(1)} %get-tuple-element.16.gv, ...), custom_call_target="tpu_custom_call" | custom-call | tf_op jit(solution)/shard_map/pallas_call | solution.py:476

commit v6 on v5

--- a/solution.py
+++ b/solution.py
@@ -107,8 +107,31 @@
     s_sems, t_sems = seq_sems[:4], seq_sems[4:]
 
     barrier = pltpu.get_barrier_semaphore()
-    for step in range(1, n_seq):
-        pl.semaphore_signal(barrier, inc=1, device_id={"seq": lax.rem(pos + step, n_seq)}, device_id_type=MESH)
+    last = n_seq - 1
+    direct = n_seq <= 4
+    merge = direct and last == 3
+    own_way = jnp.logical_not(second) if merge else True
+    ahead = not merge
+
+    def both(a, b):
+        return jnp.logical_and(a, b)
+
+    def sends(source, target):
+        to_next = both(target == source + 1, target < last if direct else True)
+        to_next_back = both(target == source - 1, target > 0 if direct else True)
+        near = jnp.logical_or(to_next, to_next_back)
+        if not direct:
+            return near
+        to_end = both(target == last, both(source < last, jnp.logical_or(source > 0, ahead)))
+        to_start = both(target == 0, both(source > 0, jnp.logical_or(source < last, own_way)))
+        return jnp.logical_or(near, jnp.logical_or(to_end, to_start))
+
+    for other in range(n_seq):
+
+        @pl.when(sends(other, pos))
+        def _():
+            pl.semaphore_signal(barrier, inc=1, device_id={"seq": other}, device_id_type=MESH)
+
     loads = [
         pltpu.make_async_copy(src, dst, in_sem.at[i])
         for i, (src, dst) in enumerate(
@@ -126,13 +149,11 @@
     def exchange(way, src, passed, near, far, sems):
         far_send, far_recv, near_send, near_recv = sems
         order = pos if way == 1 else n_seq - 1 - pos
-        last = n_seq - 1
-        direct = n_seq <= 4
         middle = jnp.logical_and(order > 0, order < (last - 1 if direct else last))
         heads_chain = jnp.logical_and(order == 0, last > (1 if direct else 0))
 
-        merge = direct and last == 3
-        merged = jnp.logical_and(second, order <= 1) if merge else False
+        skips = True if way == 1 else second
+        merged = jnp.logical_and(skips, order <= 1) if merge else False
 
         def piece(p, parts):
             return pl.ds(p * (d // parts), d // parts)
@@ -165,7 +186,7 @@
 
                 if merge:
 
-                    @pl.when(jnp.logical_and(order == last, second))
+                    @pl.when(jnp.logical_and(order == last, skips))
                     def _():
                         far[0] = jnp.zeros(far.shape[1:], F32)
 
@@ -229,7 +250,7 @@
                     for k in range(1 if merge else 0, last):
                         far_copy(k, p).wait_recv()
 
-                if merge:
+                if merge and way == -1:
 
                     @pl.when(jnp.logical_and(order == last, jnp.logical_not(second)))
                     def _():
@@ -285,7 +306,10 @@
         keep(v_in, v_h, v_l, b)
         before.append(before[-1] + outer(pair(v_h, v_l, b), pair(k_h, k_l, b)))
     send_s[...] = before[-1]
-    pl.semaphore_wait(barrier, n_head - 1 + n_seq - 1)
+    greeted = n_head - 1
+    for other in range(n_seq):
+        greeted = greeted + jnp.where(sends(pos, other), 1, 0)
+    pl.semaphore_wait(barrier, greeted)
     s_next()
     for p in range(PARTS):
         s_last(p)

time: 23.2 us -> 22.4 us (0.966)
  Pallas kernels: 21.8 us -> 21 us
    pallas_call x1, Pallas kernels: 20.6 us -> 19.8 us  [on_device(): pl.pallas_call(functools.partial(kernel, n_seq, n_head, block), out_shape...]
where the time goes in v6:
time: 22.4 us; the launch traced here: 22.2 us
  Pallas kernels  21 us (94%)
  between operations  1.29 us (6%)
    pallas_call x1, Pallas kernels, on_device(): pl.pallas_call(functools.partial(kernel, n_seq, n_head, block), out_shape...  19.8 us
    pallas_call x1, Pallas kernels, on_device(): pl.pallas_call(functools.partial(finish, block), out_shape=[rows] * 4, in...  1.2 us

profile of v6, /device:TPU:0, one launch (start us, length us, event | category | flops | bytes accessed | tf_op | source)
XLA Modules:
  0.0 22.2 jit_solution(14080329033413233396)
XLA Ops:
  1.3 19.8 %shard_map.102 = (f32[768,128]{1,0:T(8,128)S(1)}, f32[768,128]{1,0:T(8,128)S(1)}, f32[768,128]{1,0:T(8,128)S(1)}, f32[768,128]{1,0:T(8,128)S(1)}, bf16[768,128]{...) custom-call(f32[1]{0:T(128)S(6)} %copy.11.head_scale, ...), custom_call_target="tpu_custom_call" | custom-call | tf_op jit(solution)/shard_map/pallas_call | solution.py:476
  21.0 1.2 %shard_map.103 = (f32[768,128]{1,0:T(8,128)}, f32[768,128]{1,0:T(8,128)}, f32[768,128]{1,0:T(8,128)}, f32[768,128]{1,0:T(8,128)}) custom-call(f32[768,128]{1,0:T(8,128)S(1)} %get-tuple-element.13.normed, f32[768,128]{1,0:T(8,128)S(1)} %get-tuple-element.14.gq, f32[768,128]{1,0:T(8,128)S(1)} %get-tuple-element.15.gk, f32[768,128]{1,0:T(8,128)S(1)} %get-tuple-element.16.gv, ...), custom_call_target="tpu_custom_call" | custom-call | tf_op jit(solution)/shard_map/pallas_call | solution.py:500

commit v7 on v6

--- a/solution.py
+++ b/solution.py
@@ -416,7 +416,7 @@
         later = split(after[b + 1])
         gk[take(b), :] = times(pulled_t, q_b) + times_state(v_b, later)
         gv[take(b), :] = times(pair(p_h, p_l, b), o_b) + times_state_t(k_b, later)
-        if b == 1:
+        if b == min(1, blocks - 1):
             for p in range(PARTS):
                 t_relay(p, second)
 

time: 22.4 us -> 22.4 us (level)
  no operation moved by 1% of the time
where the time goes in v7:
time: 22.4 us; the launch traced here: 22.2 us
  Pallas kernels  21 us (94%)
  between operations  1.29 us (6%)
    pallas_call x1, Pallas kernels, on_device(): pl.pallas_call(functools.partial(kernel, n_seq, n_head, block), out_shape...  19.8 us
    pallas_call x1, Pallas kernels, on_device(): pl.pallas_call(functools.partial(finish, block), out_shape=[rows] * 4, in...  1.2 us

profile of v7, /device:TPU:0, one launch (start us, length us, event | category | flops | bytes accessed | tf_op | source)
XLA Modules:
  0.0 22.2 jit_solution(14080329033413233396)
XLA Ops:
  1.3 19.8 %shard_map.102 = (f32[768,128]{1,0:T(8,128)S(1)}, f32[768,128]{1,0:T(8,128)S(1)}, f32[768,128]{1,0:T(8,128)S(1)}, f32[768,128]{1,0:T(8,128)S(1)}, bf16[768,128]{...) custom-call(f32[1]{0:T(128)S(6)} %copy.11.head_scale, ...), custom_call_target="tpu_custom_call" | custom-call | tf_op jit(solution)/shard_map/pallas_call | solution.py:476
  21.0 1.2 %shard_map.103 = (f32[768,128]{1,0:T(8,128)}, f32[768,128]{1,0:T(8,128)}, f32[768,128]{1,0:T(8,128)}, f32[768,128]{1,0:T(8,128)}) custom-call(f32[768,128]{1,0:T(8,128)S(1)} %get-tuple-element.13.normed, f32[768,128]{1,0:T(8,128)S(1)} %get-tuple-element.14.gq, f32[768,128]{1,0:T(8,128)S(1)} %get-tuple-element.15.gk, f32[768,128]{1,0:T(8,128)S(1)} %get-tuple-element.16.gv, ...), custom_call_target="tpu_custom_call" | custom-call | tf_op jit(solution)/shard_map/pallas_call | solution.py:500
